TPU v7x, 32 devices: a whole 2x2x4 slice. The times are simulated.
32 devices in a mesh: dp: 8 (over z, x), tensor: 4 (over y, core).
Axes of the slice: x: 2, y: 2, z: 4, core: 2. Of those that a mesh axis runs over, the one named last changes fastest.
Arguments:
- tokens: bfloat16 [8192, 2048], P('dp'), may hold values from -6 to 6
- w_query: bfloat16 [2048, 2048], P('dp', 'tensor'), may hold values from -0.125 to 0.125
- w_key: bfloat16 [2048, 2048], P('dp', 'tensor'), may hold values from -0.125 to 0.125
- w_value: bfloat16 [2048, 4096], P('dp', 'tensor'), may hold values from -0.125 to 0.125
- w_gate: bfloat16 [2048, 4096], P('dp', 'tensor'), may hold values from -0.125 to 0.125
- w_out: bfloat16 [4096, 2048], P('tensor', 'dp'), may hold values from -0.125 to 0.125
- w_ffgate: bfloat16 [2048, 4096], P('dp', 'tensor'), may hold values from -0.125 to 0.125
- w_ffup: bfloat16 [2048, 4096], P('dp', 'tensor'), may hold values from -0.125 to 0.125
- w_down: bfloat16 [4096, 2048], P('tensor', 'dp'), may hold values from -0.125 to 0.125
- norm1_gain: bfloat16 [2048], P('dp'), may hold values from 0.5 to 1.5
- norm1_shift: bfloat16 [2048], P('dp'), may hold values from -1 to 1
- norm2_gain: bfloat16 [2048], P('dp'), may hold values from 0.5 to 1.5
- norm2_shift: bfloat16 [2048], P('dp'), may hold values from -1 to 1
- segment_ids: int32 [8192], P('dp'), may hold values from 0 to 63, never falling along the last dimension, each value on 1 to 512 neighbouring positions
- decay_index: int32 [8], P('tensor'), may hold values from 0 to 4
- cotangent: bfloat16 [8192, 2048], P('dp'), may hold values from -6 to 6
Outputs:
- block_out: bfloat16 [8192, 2048], P('dp')
- grad_tokens: float32 [8192, 2048], P('dp')
- grad_query: float32 [2048, 2048], P('dp', 'tensor')
- grad_key: float32 [2048, 2048], P('dp', 'tensor')
- grad_value: float32 [2048, 4096], P('dp', 'tensor')
- grad_gate: float32 [2048, 4096], P('dp', 'tensor')
- grad_out: float32 [4096, 2048], P('tensor', 'dp')
- grad_ffgate: float32 [2048, 4096], P('dp', 'tensor')
- grad_ffup: float32 [2048, 4096], P('dp', 'tensor')
- grad_down: float32 [4096, 2048], P('tensor', 'dp')
- grad_gain_one: float32 [2048], P('dp')
- grad_shift_one: float32 [2048], P('dp')
- grad_gain_two: float32 [2048], P('dp')
- grad_shift_two: float32 [2048], P('dp')
Inputs may be any that keep to these rules, and one draw needn't show every extreme that they name: `segment_ids`: segment numbers never fall along the tokens; a sequence boundary resets retention even where the number continues.
All inputs are finite; a program needn't handle non-finite values.
Results may differ from a plain program's by a relative error of at most 0.018.
Values may be sent and summed in bfloat16 or wider, within the bound.
No kernel may reach another device: no remote copies, remote signals or barrier semaphores. Data moves between devices by JAX's collectives and lax.ppermute only.
A program may use at most 256 MiB of HBM per device.

v0:
```python
import math
import jax
import jax.numpy as jnp
from jax import lax
from jax.sharding import PartitionSpec as P

HEAD_KEY = 256
HEAD_VALUE = 512
LENGTH = 1024
EPSILON = 1e-05
GROUP_EPSILON = 1.0
XPOS_SPAN = 512.0
INV_ROOT2 = 1.0 / math.sqrt(2.0)
INV_ROOT_TWO_PI = 1.0 / math.sqrt(2.0 * math.pi)


def xpos_tables(length, width):
    half = width // 2
    index = jnp.arange(half, dtype=jnp.float32)
    theta = jnp.exp(index * (-math.log(10000.0) / half))
    zeta = (2.0 * index + 0.4 * width) / (1.4 * width)
    position = jnp.arange(length, dtype=jnp.float32) - float(length // 2)
    angle = position[:, None] * theta[None, :]
    growth = jnp.exp(position[:, None] * (1.0 / XPOS_SPAN) * jnp.log(zeta)[None, :])
    return (jnp.cos(angle), jnp.sin(angle), growth)


def rotate(values, cosine, sine, factor):
    half = values.shape[-1] // 2
    first = values[..., :half]
    second = values[..., half:]
    cos_b = cosine[:, None, :]
    sin_b = sine[:, None, :]
    scale = factor[:, None, :]
    return jnp.concatenate(
        [(first * cos_b - second * sin_b) * scale, (second * cos_b + first * sin_b) * scale],
        axis=-1,
    )


def unrotate(grads, cosine, sine, factor):
    half = grads.shape[-1] // 2
    scale = factor[:, None, :]
    first = grads[..., :half] * scale
    second = grads[..., half:] * scale
    cos_b = cosine[:, None, :]
    sin_b = sine[:, None, :]
    return jnp.concatenate(
        [first * cos_b + second * sin_b, second * cos_b - first * sin_b], axis=-1
    )


def decay_mask(row_start, row_segment, col_segment, log_gamma):
    row_pos = row_start + jnp.arange(row_segment.shape[0], dtype=jnp.int32)
    col_pos = jnp.arange(col_segment.shape[0], dtype=jnp.int32)
    gap = row_pos[:, None] - col_pos[None, :]
    keep = (gap >= 0) & (row_segment[:, None] == col_segment[None, :])
    distance = jnp.maximum(gap, 0).astype(jnp.float32)
    return jnp.where(keep[None], jnp.exp(distance[None] * log_gamma[:, None, None]), 0.0)


def norm_parts(values, offset):
    centred = values - jnp.mean(values, axis=-1, keepdims=True)
    inv_scale = lax.rsqrt(jnp.mean(centred * centred, axis=-1, keepdims=True) + offset)
    return (centred * inv_scale, inv_scale)


def norm_back(grad_out, normed, inv_scale, gain):
    grad_norm = grad_out * gain
    return inv_scale * (
        grad_norm
        - jnp.mean(grad_norm, axis=-1, keepdims=True)
        - normed * jnp.mean(grad_norm * normed, axis=-1, keepdims=True)
    )


def retention_forward(query_rot, key_rot, values, segment, log_gamma):
    length = query_rot.shape[0]
    rows = min(512, length)
    outputs = []
    for block_start in range(0, length, rows):
        raw = jnp.einsum(
            "nhk,mhk->hnm",
            query_rot[block_start : block_start + rows],
            key_rot,
            preferred_element_type=jnp.float32,
        )
        mask = decay_mask(
            block_start, segment[block_start : block_start + rows], segment, log_gamma
        )
        weighted = (raw * mask).astype(jnp.bfloat16)
        outputs.append(
            jnp.einsum("hnm,mhv->nhv", weighted, values, preferred_element_type=jnp.float32)
        )
    return jnp.concatenate(outputs, axis=0)


def retention_backward(query_rot, key_rot, values, segment, log_gamma, grad_mixed):
    length = query_rot.shape[0]
    rows = min(512, length)
    grad_query = []
    grad_key = jnp.zeros(key_rot.shape, jnp.float32)
    grad_value = jnp.zeros(values.shape, jnp.float32)
    for block_start in range(0, length, rows):
        query_block = query_rot[block_start : block_start + rows]
        grad_block = grad_mixed[block_start : block_start + rows]
        raw = jnp.einsum("nhk,mhk->hnm", query_block, key_rot, preferred_element_type=jnp.float32)
        mask = decay_mask(
            block_start, segment[block_start : block_start + rows], segment, log_gamma
        )
        weighted = (raw * mask).astype(jnp.bfloat16)
        grad_value = grad_value + jnp.einsum(
            "hnm,nhv->mhv", weighted, grad_block, preferred_element_type=jnp.float32
        )
        grad_weighted = jnp.einsum(
            "nhv,mhv->hnm", grad_block, values, preferred_element_type=jnp.float32
        )
        grad_raw = (grad_weighted * mask).astype(jnp.bfloat16)
        grad_query.append(
            jnp.einsum("hnm,mhk->nhk", grad_raw, key_rot, preferred_element_type=jnp.float32)
        )
        grad_key = grad_key + jnp.einsum(
            "hnm,nhk->mhk", grad_raw, query_block, preferred_element_type=jnp.float32
        )
    return (jnp.concatenate(grad_query, axis=0), grad_key, grad_value)


def dense(left, right):
    return jnp.dot(left, right, preferred_element_type=jnp.float32)


def local(
    tokens,
    w_query,
    w_key,
    w_value,
    w_gate,
    w_out,
    w_ffgate,
    w_ffup,
    w_down,
    norm1_gain,
    norm1_shift,
    norm2_gain,
    norm2_shift,
    segment_ids,
    decay_index,
    cotangent,
):
    gathered = (
        lax.all_gather(w_query, "dp", axis=0, tiled=True),
        lax.all_gather(w_key, "dp", axis=0, tiled=True),
        lax.all_gather(w_value, "dp", axis=0, tiled=True),
        lax.all_gather(w_gate, "dp", axis=0, tiled=True),
        lax.all_gather(w_out, "dp", axis=1, tiled=True),
        lax.all_gather(w_ffgate, "dp", axis=0, tiled=True),
        lax.all_gather(w_ffup, "dp", axis=0, tiled=True),
        lax.all_gather(w_down, "dp", axis=1, tiled=True),
        lax.all_gather(norm1_gain, "dp", axis=0, tiled=True),
        lax.all_gather(norm1_shift, "dp", axis=0, tiled=True),
        lax.all_gather(norm2_gain, "dp", axis=0, tiled=True),
        lax.all_gather(norm2_shift, "dp", axis=0, tiled=True),
    )
    (
        full_query,
        full_key,
        full_value,
        full_gate,
        full_out,
        full_ffgate,
        full_ffup,
        full_down,
        gain_one,
        shift_one,
        gain_two,
        shift_two,
    ) = gathered
    count = tokens.shape[0]
    seqs = count // LENGTH
    heads = full_query.shape[1] // HEAD_KEY
    inputs = tokens.astype(jnp.float32)
    log_gamma = jnp.log1p(-jnp.exp2(-5.0 - decay_index.astype(jnp.float32)))
    normed_one, scale_one = norm_parts(inputs, EPSILON)
    first_in = (normed_one * gain_one.astype(jnp.float32) + shift_one.astype(jnp.float32)).astype(
        jnp.bfloat16
    )
    query = dense(first_in, full_query).reshape(seqs, LENGTH, heads, HEAD_KEY)
    keys = dense(first_in, full_key).reshape(seqs, LENGTH, heads, HEAD_KEY)
    values_seq = (
        dense(first_in, full_value).astype(jnp.bfloat16).reshape(seqs, LENGTH, heads, HEAD_VALUE)
    )
    gate = dense(first_in, full_gate)
    cosine, sine, growth = xpos_tables(LENGTH, HEAD_KEY)
    query_rot = rotate(query, cosine, sine, growth).astype(jnp.bfloat16)
    key_rot = (rotate(keys, cosine, sine, 1.0 / growth) * HEAD_KEY ** (-0.5)).astype(jnp.bfloat16)
    segments = segment_ids.reshape(seqs, LENGTH)
    mixed = lax.map(
        lambda item: retention_forward(item[0], item[1], item[2], item[3], log_gamma),
        (query_rot, key_rot, values_seq, segments),
    )
    grouped, group_scale = norm_parts(mixed.reshape(count, heads, HEAD_VALUE), GROUP_EPSILON)
    grouped_flat = grouped.reshape(count, heads * HEAD_VALUE)
    sigmoid_gate = jax.nn.sigmoid(gate)
    swish = gate * sigmoid_gate
    gated = (swish * grouped_flat).astype(jnp.bfloat16)
    attention = lax.psum(dense(gated, full_out), "tensor")
    middle = inputs + attention
    normed_two, scale_two = norm_parts(middle, EPSILON)
    second_in = (normed_two * gain_two.astype(jnp.float32) + shift_two.astype(jnp.float32)).astype(
        jnp.bfloat16
    )
    ff_gate = dense(second_in, full_ffgate)
    ff_up = dense(second_in, full_ffup)
    normal_cdf = 0.5 * (1.0 + lax.erf(ff_gate * INV_ROOT2))
    activation = ff_gate * normal_cdf
    hidden = (activation * ff_up).astype(jnp.bfloat16)
    feed = lax.psum(dense(hidden, full_down).astype(jnp.bfloat16), "tensor").astype(jnp.float32)
    block_out = (middle + feed).astype(jnp.bfloat16)
    again = (
        lax.all_gather(w_query, "dp", axis=0, tiled=True),
        lax.all_gather(w_key, "dp", axis=0, tiled=True),
        lax.all_gather(w_value, "dp", axis=0, tiled=True),
        lax.all_gather(w_gate, "dp", axis=0, tiled=True),
        lax.all_gather(w_out, "dp", axis=1, tiled=True),
        lax.all_gather(w_ffgate, "dp", axis=0, tiled=True),
        lax.all_gather(w_ffup, "dp", axis=0, tiled=True),
        lax.all_gather(w_down, "dp", axis=1, tiled=True),
        lax.all_gather(norm1_gain, "dp", axis=0, tiled=True),
        lax.all_gather(norm1_shift, "dp", axis=0, tiled=True),
        lax.all_gather(norm2_gain, "dp", axis=0, tiled=True),
        lax.all_gather(norm2_shift, "dp", axis=0, tiled=True),
    )
    (
        back_query,
        back_key,
        back_value,
        back_gate,
        back_out,
        back_ffgate,
        back_ffup,
        back_down,
        back_gain_one,
        back_shift_one,
        back_gain_two,
        back_shift_two,
    ) = again
    grad_result = cotangent.astype(jnp.float32)
    grad_feed = grad_result.astype(jnp.bfloat16)
    grad_down = dense(hidden.T, grad_feed)
    grad_hidden = dense(grad_feed, back_down.T)
    density = jnp.exp(-0.5 * ff_gate * ff_gate) * INV_ROOT_TWO_PI
    grad_ffgate_in = (grad_hidden * ff_up * (normal_cdf + ff_gate * density)).astype(jnp.bfloat16)
    grad_ffup_in = (grad_hidden * activation).astype(jnp.bfloat16)
    grad_ffgate = dense(second_in.T, grad_ffgate_in)
    grad_ffup = dense(second_in.T, grad_ffup_in)
    grad_second = lax.psum(
        dense(grad_ffgate_in, back_ffgate.T) + dense(grad_ffup_in, back_ffup.T), "tensor"
    )
    grad_gain_two = jnp.sum(grad_second * normed_two, axis=0)
    grad_shift_two = jnp.sum(grad_second, axis=0)
    grad_middle = grad_result + norm_back(
        grad_second, normed_two, scale_two, back_gain_two.astype(jnp.float32)
    )
    grad_branch = grad_middle.astype(jnp.bfloat16)
    grad_out = dense(gated.T, grad_branch)
    grad_gated = dense(grad_branch, back_out.T)
    swish_slope = sigmoid_gate * (1.0 + gate * (1.0 - sigmoid_gate))
    grad_gate_in = (grad_gated * grouped_flat * swish_slope).astype(jnp.bfloat16)
    grad_grouped = (grad_gated * swish).reshape(count, heads, HEAD_VALUE)
    grad_mixed = norm_back(grad_grouped, grouped, group_scale, 1.0).astype(jnp.bfloat16)
    grad_mixed_seq = grad_mixed.reshape(seqs, LENGTH, heads, HEAD_VALUE)
    grad_qrot, grad_krot, grad_values = lax.map(
        lambda item: retention_backward(item[0], item[1], item[2], item[3], log_gamma, item[4]),
        (query_rot, key_rot, values_seq, segments, grad_mixed_seq),
    )
    grad_query_in = (
        unrotate(grad_qrot, cosine, sine, growth)
        .astype(jnp.bfloat16)
        .reshape(count, heads * HEAD_KEY)
    )
    grad_key_in = (
        (unrotate(grad_krot, cosine, sine, 1.0 / growth) * HEAD_KEY ** (-0.5))
        .astype(jnp.bfloat16)
        .reshape(count, heads * HEAD_KEY)
    )
    grad_value_in = grad_values.astype(jnp.bfloat16).reshape(count, heads * HEAD_VALUE)
    grad_query = dense(first_in.T, grad_query_in)
    grad_key = dense(first_in.T, grad_key_in)
    grad_value = dense(first_in.T, grad_value_in)
    grad_gate = dense(first_in.T, grad_gate_in)
    partial_first = (
        dense(grad_query_in, back_query.T)
        + dense(grad_key_in, back_key.T)
        + dense(grad_value_in, back_value.T)
        + dense(grad_gate_in, back_gate.T)
    )
    grad_first = lax.psum(partial_first.astype(jnp.bfloat16), "tensor").astype(jnp.float32)
    grad_gain_one = jnp.sum(grad_first * normed_one, axis=0)
    grad_shift_one = jnp.sum(grad_first, axis=0)
    grad_tokens = grad_middle + norm_back(
        grad_first, normed_one, scale_one, back_gain_one.astype(jnp.float32)
    )
    shares = tuple(
        (
            lax.psum_scatter(grad_query, "dp", scatter_dimension=0, tiled=True),
            lax.psum_scatter(grad_key, "dp", scatter_dimension=0, tiled=True),
            lax.psum_scatter(grad_value, "dp", scatter_dimension=0, tiled=True),
            lax.psum_scatter(grad_gate, "dp", scatter_dimension=0, tiled=True),
            lax.psum_scatter(grad_out, "dp", scatter_dimension=1, tiled=True),
            lax.psum_scatter(grad_ffgate, "dp", scatter_dimension=0, tiled=True),
            lax.psum_scatter(grad_ffup, "dp", scatter_dimension=0, tiled=True),
            lax.psum_scatter(grad_down, "dp", scatter_dimension=1, tiled=True),
            lax.psum_scatter(grad_gain_one, "dp", scatter_dimension=0, tiled=True),
            lax.psum_scatter(grad_shift_one, "dp", scatter_dimension=0, tiled=True),
            lax.psum_scatter(grad_gain_two, "dp", scatter_dimension=0, tiled=True),
            lax.psum_scatter(grad_shift_two, "dp", scatter_dimension=0, tiled=True),
        )
    )
    return (block_out, grad_tokens) + shares


def solution(mesh):
    placed = (
        P("dp", None),
        P("dp", "tensor"),
        P("dp", "tensor"),
        P("dp", "tensor"),
        P("dp", "tensor"),
        P("tensor", "dp"),
        P("dp", "tensor"),
        P("dp", "tensor"),
        P("tensor", "dp"),
        P("dp"),
        P("dp"),
        P("dp"),
        P("dp"),
        P("dp"),
        P("tensor"),
        P("dp", None),
    )
    return jax.shard_map(
        local,
        mesh=mesh,
        in_specs=placed,
        out_specs=(
            P("dp", None),
            P("dp", None),
            P("dp", "tensor"),
            P("dp", "tensor"),
            P("dp", "tensor"),
            P("dp", "tensor"),
            P("tensor", "dp"),
            P("dp", "tensor"),
            P("dp", "tensor"),
            P("tensor", "dp"),
            P("dp"),
            P("dp"),
            P("dp"),
            P("dp"),
        ),
        check_vma=False,
    )
```

profile of v0, /device:TPU:0, one launch (start us, length us, event | category | flops | bytes accessed | tf_op | source)
XLA Modules:
  0.0 2234.8 jit_solution(5405685063912232103)
XLA Ops:
  19.0 22.3 all-gather
  41.4 16.7 all-gather.1
  76.4 35.5 %all-gather.19.cloned.1.call-done = bf16[2048,512]{1,0:T(8,128)(2,1)} async-done(((bf16[256,512]{1,0:T(8,128)(2,1)}), bf16[2048,512]{1,0:T(8,128)(2,1)}) %all-gather.19.cloned.1.call-update) | async-done | bytes 2097168 | tf_op jit(solution)/shard_map/all_gather | solution.py:152
  132.1 53.3 %all-gather.15.cloned.1.call-done = bf16[2048,1024]{1,0:T(8,128)(2,1)} async-done(((bf16[256,1024]{1,0:T(8,128)(2,1)}), bf16[2048,1024]{1,0:T(8,128)(2,1)}) %all-gather.15.cloned.1.call-update) | async-done | bytes 4194320 | tf_op jit(solution)/shard_map/all_gather | solution.py:153
  185.4 8.4 convolution_convert_fusion.1
  198.9 59.9 %all-gather.13.cloned.1.call-done = bf16[2048,1024]{1,0:T(8,128)(2,1)} async-done(((bf16[256,1024]{1,0:T(8,128)(2,1)}), bf16[2048,1024]{1,0:T(8,128)(2,1)}) %all-gather.13.cloned.1.call-update) | async-done | bytes 4194320 | tf_op jit(solution)/shard_map/all_gather | solution.py:154
  258.8 12.2 multiply_convert_fusion.5
  271.0 62.9 %all-gather.21.cloned.1.call-done = bf16[1024,2048]{1,0:T(8,128)(2,1)} async-done(((bf16[1024,256]{1,0:T(8,128)(2,1)}), bf16[1024,2048]{1,0:T(8,128)(2,1)}) %all-gather.21.cloned.1.call-update) | async-done | bytes 4194320 | tf_op jit(solution)/shard_map/all_gather | solution.py:155
  333.9 11.0 fusion.63
  347.2 17.7 all-gather.2
  365.0 16.9 all-gather.3
  381.9 114.3 %all-reduce.10.cloned.1.call-done = f32[1024,2048]{1,0:T(8,128)} async-done(((f32[1024,2048]{1,0:T(8,128)}), f32[1024,2048]{1,0:T(8,128)}) %all-reduce.10.cloned.1.call-update) | async-done | bytes 8388624 | tf_op jit(solution)/shard_map/psum | solution.py:206
  508.0 63.2 %all-gather.23.cloned.1.call-done = bf16[2048,1024]{1,0:T(8,128)(2,1)} async-done(((bf16[256,1024]{1,0:T(8,128)(2,1)}), bf16[2048,1024]{1,0:T(8,128)(2,1)}) %all-gather.23.cloned.1.call-update) | async-done | bytes 4194320 | tf_op jit(solution)/shard_map/all_gather | solution.py:156
  571.2 10.0 fusion.64
  581.2 63.5 %all-gather.25.cloned.1.call-done = bf16[2048,1024]{1,0:T(8,128)(2,1)} async-done(((bf16[256,1024]{1,0:T(8,128)(2,1)}), bf16[2048,1024]{1,0:T(8,128)(2,1)}) %all-gather.25.cloned.1.call-update) | async-done | bytes 4194320 | tf_op jit(solution)/shard_map/all_gather | solution.py:157
  644.7 10.0 fusion.65
  654.7 65.2 %all-gather.27.cloned.1.call-done = bf16[1024,2048]{1,0:T(8,128)(2,1)} async-done(((bf16[1024,256]{1,0:T(8,128)(2,1)}), bf16[1024,2048]{1,0:T(8,128)(2,1)}) %all-gather.27.cloned.1.call-update) | async-done | bytes 4194320 | tf_op jit(solution)/shard_map/all_gather | solution.py:158
  719.9 12.7 multiply_convert_fusion.3
  737.3 6.9 convolution_add_fusion
  744.5 9.4 convolution_convert_fusion
  753.9 141.5 %all-reduce.12.cloned.1.call-done = f32[1024,2048]{1,0:T(8,128)} async-done(((f32[1024,2048]{1,0:T(8,128)}), f32[1024,2048]{1,0:T(8,128)}) %all-reduce.12.cloned.1.call-update) | async-done | bytes 8388624 | tf_op jit(solution)/shard_map/psum | solution.py:256
  895.5 8.3 multiply_reduce_fusion
  903.8 7.5 multiply_add_fusion
  911.5 13.1 multiply_convert_fusion
  959.0 6.9 fusion.68
  965.9 6.9 fusion.69
  972.7 11.4 add_convert_fusion
  984.4 6.7 fusion.71
  992.3 6.5 fusion.70
  1000.5 9.1 fusion.74
  1011.2 9.1 fusion.75
  1022.1 8.8 fusion.76
  1032.5 10.1 fusion.29
  1044.2 9.1 fusion.72
  1054.8 9.1 fusion.73
  1065.8 71.5 %all-reduce.14.cloned.1.call-done = (bf16[1024,2048]{1,0:T(8,128)(2,1)}, bf16[1024,2048]{1,0:T(8,128)(2,1)}) async-done(((bf16[1024,2048]{1,0:T(8,128)(2,1)}, bf16[1024,2048]{1,0:T(8,128)(2,1)}), (bf16[1024,2048]{1,0:T(8,128)(2,1)}, bf16[1024,2048]{1,0:T(8,128)(2,1)})) %all-reduce.14.cloned.1.call-update) | async-done | bytes 8388624 | tf_op jit(solution)/shard_map/psum | solution.py:217
  1137.3 6.2 fusion.14
  1143.6 39.5 %all-reduce.4 = (f32[2048]{0:T(1024)S(1)}, f32[2048]{0:T(1024)S(1)}, f32[2048]{0:T(1024)S(1)}, f32[2048]{0:T(1024)S(1)}) all-reduce(f32[2048]{0:T(1024)S(1)} %get-tuple-element.68, f32[2048]{0:T(1024)S(1)} %get-tuple-element.72, f32[2048]{0:T(1024)S(1)} %copy-done.48, ...), channel_id=10, replica_groups=mesh['dp'=8,'tensor'=4] {'dp'}, use_global_device_ids=true, to_apply=%region_25.26.clone | all-reduce | flops 8192 | bytes 65536
  1185.6 8.5 add_convert_fusion.1
  1194.1 7.4 fusion.11
  1201.5 28.9 %reduce-scatter.11.cloned.1.call-done = f32[256,512]{1,0:T(8,128)} async-done(((f32[2048,512]{1,0:T(8,128)}), f32[256,512]{1,0:T(8,128)}) %reduce-scatter.11.cloned.1.call-update) | async-done | bytes 524304 | tf_op jit(solution)/shard_map/reduce_scatter | solution.py:306
  1230.4 92.2 %reduce-scatter.9.cloned.1.call-done = f32[256,512]{1,0:T(8,128)} async-done(((f32[2048,512]{1,0:T(8,128)}), f32[256,512]{1,0:T(8,128)}) %reduce-scatter.9.cloned.1.call-update) | async-done | bytes 524304 | tf_op jit(solution)/shard_map/reduce_scatter | solution.py:305
  1322.6 151.2 %reduce-scatter.19.cloned.1.call-done = f32[256,1024]{1,0:T(8,128)} async-done(((f32[2048,1024]{1,0:T(8,128)}), f32[256,1024]{1,0:T(8,128)}) %reduce-scatter.19.cloned.1.call-update) | async-done | bytes 1048592 | tf_op jit(solution)/shard_map/reduce_scatter | solution.py:310
  1473.8 150.6 %reduce-scatter.21.cloned.1.call-done = f32[256,1024]{1,0:T(8,128)} async-done(((f32[2048,1024]{1,0:T(8,128)}), f32[256,1024]{1,0:T(8,128)}) %reduce-scatter.21.cloned.1.call-update) | async-done | bytes 1048592 | tf_op jit(solution)/shard_map/reduce_scatter | solution.py:311
  1624.4 151.0 %reduce-scatter.23.cloned.1.call-done = f32[1024,256]{1,0:T(8,128)} async-done(((f32[1024,2048]{1,0:T(8,128)}), f32[1024,256]{1,0:T(8,128)}) %reduce-scatter.23.cloned.1.call-update) | async-done | bytes 1048592 | tf_op jit(solution)/shard_map/reduce_scatter | solution.py:312
  1775.5 151.1 %reduce-scatter.17.cloned.1.call-done = f32[1024,256]{1,0:T(8,128)} async-done(((f32[1024,2048]{1,0:T(8,128)}), f32[1024,256]{1,0:T(8,128)}) %reduce-scatter.17.cloned.1.call-update) | async-done | bytes 1048592 | tf_op jit(solution)/shard_map/reduce_scatter | solution.py:309
  1926.5 150.7 %reduce-scatter.13.cloned.1.call-done = f32[256,1024]{1,0:T(8,128)} async-done(((f32[2048,1024]{1,0:T(8,128)}), f32[256,1024]{1,0:T(8,128)}) %reduce-scatter.13.cloned.1.call-update) | async-done | bytes 1048592 | tf_op jit(solution)/shard_map/reduce_scatter | solution.py:307
  2077.2 150.8 %reduce-scatter.15.cloned.1.call-done = f32[256,1024]{1,0:T(8,128)} async-done(((f32[2048,1024]{1,0:T(8,128)}), f32[256,1024]{1,0:T(8,128)}) %reduce-scatter.15.cloned.1.call-update) | async-done | bytes 1048592 | tf_op jit(solution)/shard_map/reduce_scatter | solution.py:308
  (251 shorter events, 123.2 us)
Async XLA Ops:
  7.2 58.3 %all-gather.17.cloned.1.call-start = ((), (), s32[]{:S(2)}) async-start(), calls=%async_computation.10 | async-start | bytes 2359296 | tf_op jit(solution)/shard_map/all_gather | solution.py:151
  7.9 104.0 %all-gather.19.cloned.1.call-start = ((), (), s32[]{:S(2)}) async-start(), calls=%async_computation.11 | async-start | bytes 2359296 | tf_op jit(solution)/shard_map/all_gather | solution.py:152
  8.7 176.8 %all-gather.15.cloned.1.call-start = ((), (), s32[]{:S(2)}) async-start(), calls=%async_computation.9 | async-start | bytes 4718592 | tf_op jit(solution)/shard_map/all_gather | solution.py:153
  9.4 249.4 %all-gather.13.cloned.1.call-start = ((), (), s32[]{:S(2)}) async-start(), calls=%async_computation.8 | async-start | bytes 4718592 | tf_op jit(solution)/shard_map/all_gather | solution.py:154
  10.0 323.9 %all-gather.21.cloned.1.call-start = ((), (), s32[]{:S(2)}) async-start(), calls=%async_computation.12 | async-start | bytes 4718592 | tf_op jit(solution)/shard_map/all_gather | solution.py:155
  10.6 485.6 %all-reduce.10.cloned.1.call-start = ((), (), s32[]{:S(2)}) async-start(), calls=%async_computation.13 | async-start | bytes 16777216 | tf_op jit(solution)/shard_map/psum | solution.py:206
  10.6 4.9 copy-start.1
  15.5 25.8 %copy-start.57 = (bf16[256]{0:T(256)(128)(2,1)S(1)}, bf16[256]{0:T(256)(128)(2,1)}, u32[]{:S(2)}) copy-start(bf16[256]{0:T(256)(128)(2,1)} %param.26) | copy-start | bytes 1540
  15.5 46.3 %copy-start.44 = (f32[1024]{0:T(1024)}, f32[1024]{0:T(1024)S(1)}, u32[]{:S(2)}) copy-start(f32[1024]{0:T(1024)S(1)} %broadcast_multiply_fusion.9) | copy-start | bytes 12292
  16.8 45.1 %copy-start.46 = (f32[1024]{0:T(1024)}, f32[1024]{0:T(1024)S(1)}, u32[]{:S(2)}) copy-start(f32[1024]{0:T(1024)S(1)} %add_rsqrt_fusion.2) | copy-start | bytes 12292
  17.0 106.9 %copy-start.14 = (f32[1024,128]{1,0:T(8,128)}, f32[1024,128]{1,0:T(8,128)S(1)}, u32[]{:S(2)}) copy-start(f32[1024,128]{1,0:T(8,128)S(1)} %get-tuple-element.103) | copy-start | bytes 1572868
  17.1 106.9 %copy-start.16 = (f32[1024,128]{1,0:T(8,128)}, f32[1024,128]{1,0:T(8,128)S(1)}, u32[]{:S(2)}) copy-start(f32[1024,128]{1,0:T(8,128)S(1)} %get-tuple-element.104) | copy-start | bytes 1572868
  19.0 105.0 %copy-start.18 = (f32[1024,128]{1,0:T(8,128)}, f32[1024,128]{1,0:T(8,128)S(1)}, u32[]{:S(2)}) copy-start(f32[1024,128]{1,0:T(8,128)S(1)} %get-tuple-element.105) | copy-start | bytes 1572868
  19.0 105.0 %copy-start.20 = (f32[1024,128]{1,0:T(8,128)}, f32[1024,128]{1,0:T(8,128)S(1)}, u32[]{:S(2)}) copy-start(f32[1024,128]{1,0:T(8,128)S(1)} %get-tuple-element.106) | copy-start | bytes 1572868
  41.3 20.5 copy-start.42
  185.4 8.4 copy-start.26
  344.9 20.1 copy-start.59
  344.9 226.3 %all-gather.23.cloned.1.call-start = ((), (), s32[]{:S(2)}) async-start(), calls=%async_computation.14 | async-start | bytes 4718592 | tf_op jit(solution)/shard_map/all_gather | solution.py:156
  345.7 299.0 %all-gather.25.cloned.1.call-start = ((), (), s32[]{:S(2)}) async-start(), calls=%async_computation.15 | async-start | bytes 4718592 | tf_op jit(solution)/shard_map/all_gather | solution.py:157
  346.4 373.5 %all-gather.27.cloned.1.call-start = ((), (), s32[]{:S(2)}) async-start(), calls=%async_computation.16 | async-start | bytes 4718592 | tf_op jit(solution)/shard_map/all_gather | solution.py:158
  347.1 548.3 %all-reduce.12.cloned.1.call-start = ((), (), s32[]{:S(2)}) async-start(), calls=%async_computation.17 | async-start | bytes 16777216 | tf_op jit(solution)/shard_map/psum | solution.py:256
  719.9 12.7 copy-start.52
  732.7 4.6 copy-start.64
  732.7 4.6 copy-start.53
  744.3 393.0 %all-reduce.14.cloned.1.call-start = ((), (), s32[]{:S(2)}) async-start(), calls=%async_computation.26 | async-start | bytes 16777216 | tf_op jit(solution)/shard_map/psum | solution.py:217
  895.5 8.3 copy-start.23
  903.8 7.5 copy-start.5
  903.8 7.7 copy-start.6
  911.3 13.2 copy-start.3
  930.5 6.4 copy-start.8
  944.2 7.6 copy-start.9
  959.0 6.9 copy-start.22
  959.0 6.9 copy-start.24
  984.1 246.3 %reduce-scatter.11.cloned.1.call-start = ((), (), s32[]{:S(2)}) async-start(), calls=%async_computation.19 | async-start | bytes 4718592 | tf_op jit(solution)/shard_map/reduce_scatter | solution.py:306
  991.1 331.5 %reduce-scatter.9.cloned.1.call-start = ((), (), s32[]{:S(2)}) async-start(), calls=%async_computation.18 | async-start | bytes 4718592 | tf_op jit(solution)/shard_map/reduce_scatter | solution.py:305
  998.9 474.9 %reduce-scatter.19.cloned.1.call-start = ((), (), s32[]{:S(2)}) async-start(), calls=%async_computation.23 | async-start | bytes 9437184 | tf_op jit(solution)/shard_map/reduce_scatter | solution.py:310
  1009.6 614.8 %reduce-scatter.21.cloned.1.call-start = ((), (), s32[]{:S(2)}) async-start(), calls=%async_computation.24 | async-start | bytes 9437184 | tf_op jit(solution)/shard_map/reduce_scatter | solution.py:311
  1020.4 755.1 %reduce-scatter.23.cloned.1.call-start = ((), (), s32[]{:S(2)}) async-start(), calls=%async_computation.25 | async-start | bytes 9437184 | tf_op jit(solution)/shard_map/reduce_scatter | solution.py:312
  1030.9 895.6 %reduce-scatter.17.cloned.1.call-start = ((), (), s32[]{:S(2)}) async-start(), calls=%async_computation.22 | async-start | bytes 9437184 | tf_op jit(solution)/shard_map/reduce_scatter | solution.py:309
  1042.6 1034.6 %reduce-scatter.13.cloned.1.call-start = ((), (), s32[]{:S(2)}) async-start(), calls=%async_computation.20 | async-start | bytes 9437184 | tf_op jit(solution)/shard_map/reduce_scatter | solution.py:307
  1053.3 1174.7 %reduce-scatter.15.cloned.1.call-start = ((), (), s32[]{:S(2)}) async-start(), calls=%async_computation.21 | async-start | bytes 9437184 | tf_op jit(solution)/shard_map/reduce_scatter | solution.py:308
  1064.0 73.4 %copy-start.43 = (f32[8,1,256]{2,1,0:T(1,128)S(1)}, f32[8,1,256]{2,1,0:T(1,128)}, u32[]{:S(2)}) copy-start(f32[8,1,256]{2,1,0:T(1,128)} %copy-done.42) | copy-start | bytes 24580
  1064.0 73.4 %copy-start.45 = (f32[1024]{0:T(1024)S(1)}, f32[1024]{0:T(1024)}, u32[]{:S(2)}) copy-start(f32[1024]{0:T(1024)} %copy-done.44) | copy-start | bytes 12292
  1064.0 73.4 %copy-start.47 = (f32[1024]{0:T(1024)S(1)}, f32[1024]{0:T(1024)}, u32[]{:S(2)}) copy-start(f32[1024]{0:T(1024)} %copy-done.46) | copy-start | bytes 12292
  1137.3 6.2 copy-start.48
  1137.3 6.2 copy-start.49
  1185.6 8.5 copy-start.2
  1185.6 8.5 copy-start.7
  (39 other events, 92.5 us)
Sparse Core Ops, SparseCore 0:
  10.1 52.0 all-gather.16
  64.3 47.5 all-gather.18
  114.1 71.3 all-gather.14
  187.4 71.3 all-gather.12
  260.6 73.1 all-gather.20
  345.0 151.0 all-reduce.9
  498.2 72.9 all-gather.22
  573.3 71.3 all-gather.24
  646.7 73.1 all-gather.26
  744.4 151.0 all-reduce.11
  984.3 153.0 all-reduce.13
  1141.4 88.9 reduce-scatter.10
  1234.6 87.9 reduce-scatter.8
  1326.6 147.0 reduce-scatter.18
  1477.8 146.5 reduce-scatter.20
  1628.5 146.9 reduce-scatter.22
  1779.5 146.9 reduce-scatter.16
  1930.6 146.5 reduce-scatter.12
  2081.4 146.5 reduce-scatter.14
where the time goes:
time: 2240 us; the launch traced here: 2230 us
  waiting for transfers between devices  1760 us (79%)
  matrix products  227 us (10%)
  blocking collectives  113 us (5%)
  other arithmetic  76.6 us (3%)
  local copies, waits for them, and re-layouts  38.1 us (2%)
    dot_general x24, matrix products, dense(): return jnp.dot(left, right, preferred_element_type=jnp.float32)  205 us
    reduce_scatter x1, waiting for transfers between devices, local(): lax.psum_scatter(grad_ffgate, 'dp', scatter_dimension=0, tiled=True)  151 us
    reduce_scatter x1, waiting for transfers between devices, local(): lax.psum_scatter(grad_out, 'dp', scatter_dimension=1, tiled=True)  151 us
    reduce_scatter x1, waiting for transfers between devices, local(): lax.psum_scatter(grad_down, 'dp', scatter_dimension=1, tiled=True)  151 us
    reduce_scatter x1, waiting for transfers between devices, local(): lax.psum_scatter(grad_gate, 'dp', scatter_dimension=0, tiled=True)  151 us
    reduce_scatter x1, waiting for transfers between devices, local(): lax.psum_scatter(grad_value, 'dp', scatter_dimension=0, tiled=True)  151 us
    reduce_scatter x1, waiting for transfers between devices, local(): lax.psum_scatter(grad_ffup, 'dp', scatter_dimension=0, tiled=True)  151 us
    psum x1, waiting for transfers between devices, local(): lax.psum(dense(grad_ffgate_in, back_ffgate.T) + dense(grad_ffup_in, back_...  142 us
  transfers between devices with their start and end apart: 19, of which 18 were waited for; matrix products, arithmetic and copies ran while one was open for 9% of the time, Pallas kernels for 0%

commit v1 on v0

--- a/solution.py
+++ b/solution.py
@@ -203,7 +203,7 @@
     sigmoid_gate = jax.nn.sigmoid(gate)
     swish = gate * sigmoid_gate
     gated = (swish * grouped_flat).astype(jnp.bfloat16)
-    attention = lax.psum(dense(gated, full_out), "tensor")
+    attention = jnp.sum(lax.all_gather(dense(gated, full_out), "tensor"), axis=0)
     middle = inputs + attention
     normed_two, scale_two = norm_parts(middle, EPSILON)
     second_in = (normed_two * gain_two.astype(jnp.float32) + shift_two.astype(jnp.float32)).astype(

time: 2240 us -> 2290 us (1.022)
  waiting for transfers between devices: 1760 us -> 1790 us
    all_gather x0 -> x1, waiting for transfers between devices: none -> 163 us  [local(): lax.all_gather(dense(gated, full_out), 'tensor')]
    psum x1 -> x0, waiting for transfers between devices: 114 us -> none  [local(): attention = lax.psum(dense(gated, full_out), 'tensor')]
  transfers between devices with their start and end apart: 19 -> 19, of which waited for: 18 -> 18; matrix products, arithmetic and copies ran while one was open for 9% -> 10% of each run, Pallas kernels for 0% -> 0%
where the time goes in v1:
time: 2290 us; the launch traced here: 2280 us
  waiting for transfers between devices  1790 us (78%)
  matrix products  227 us (10%)
  blocking collectives  113 us (5%)
  other arithmetic  92.8 us (4%)
  local copies, waits for them, and re-layouts  38.2 us (2%)
    dot_general x24, matrix products, dense(): return jnp.dot(left, right, preferred_element_type=jnp.float32)  205 us
    all_gather x1, waiting for transfers between devices, local(): lax.all_gather(dense(gated, full_out), 'tensor')  163 us
    reduce_scatter x1, waiting for transfers between devices, local(): lax.psum_scatter(grad_ffgate, 'dp', scatter_dimension=0, tiled=True)  151 us
    reduce_scatter x1, waiting for transfers between devices, local(): lax.psum_scatter(grad_out, 'dp', scatter_dimension=1, tiled=True)  151 us
    reduce_scatter x1, waiting for transfers between devices, local(): lax.psum_scatter(grad_down, 'dp', scatter_dimension=1, tiled=True)  151 us
    reduce_scatter x1, waiting for transfers between devices, local(): lax.psum_scatter(grad_gate, 'dp', scatter_dimension=0, tiled=True)  151 us
    reduce_scatter x1, waiting for transfers between devices, local(): lax.psum_scatter(grad_value, 'dp', scatter_dimension=0, tiled=True)  151 us
    reduce_scatter x1, waiting for transfers between devices, local(): lax.psum_scatter(grad_ffup, 'dp', scatter_dimension=0, tiled=True)  151 us
  transfers between devices with their start and end apart: 19, of which 18 were waited for; matrix products, arithmetic and copies ran while one was open for 10% of the time, Pallas kernels for 0%

profile of v1, /device:TPU:0, one launch (start us, length us, event | category | flops | bytes accessed | tf_op | source)
XLA Modules:
  0.0 2283.1 jit_solution(3459970912912741712)
XLA Ops:
  19.0 22.3 all-gather.1
  41.4 16.7 all-gather.2
  76.1 35.8 %all-gather.21.cloned.1.call-done = bf16[2048,512]{1,0:T(8,128)(2,1)} async-done(((bf16[256,512]{1,0:T(8,128)(2,1)}), bf16[2048,512]{1,0:T(8,128)(2,1)}) %all-gather.21.cloned.1.call-update) | async-done | bytes 2097168 | tf_op jit(solution)/shard_map/all_gather | solution.py:152
  132.2 53.2 %all-gather.17.cloned.1.call-done = bf16[2048,1024]{1,0:T(8,128)(2,1)} async-done(((bf16[256,1024]{1,0:T(8,128)(2,1)}), bf16[2048,1024]{1,0:T(8,128)(2,1)}) %all-gather.17.cloned.1.call-update) | async-done | bytes 4194320 | tf_op jit(solution)/shard_map/all_gather | solution.py:153
  185.4 8.6 convolution_convert_fusion.1
  199.2 59.6 %all-gather.15.cloned.1.call-done = bf16[2048,1024]{1,0:T(8,128)(2,1)} async-done(((bf16[256,1024]{1,0:T(8,128)(2,1)}), bf16[2048,1024]{1,0:T(8,128)(2,1)}) %all-gather.15.cloned.1.call-update) | async-done | bytes 4194320 | tf_op jit(solution)/shard_map/all_gather | solution.py:154
  258.8 12.3 multiply_convert_fusion.5
  271.0 62.8 %all-gather.23.cloned.1.call-done = bf16[1024,2048]{1,0:T(8,128)(2,1)} async-done(((bf16[1024,256]{1,0:T(8,128)(2,1)}), bf16[1024,2048]{1,0:T(8,128)(2,1)}) %all-gather.23.cloned.1.call-update) | async-done | bytes 4194320 | tf_op jit(solution)/shard_map/all_gather | solution.py:155
  333.9 11.0 fusion.63
  347.2 17.7 all-gather.3
  365.0 16.8 all-gather.4
  381.8 162.9 %all-gather.31.cloned.1.call-done = f32[4096,2048]{1,0:T(8,128)} async-done(((f32[1024,2048]{1,0:T(8,128)}), f32[4096,2048]{1,0:T(8,128)}) %all-gather.31.cloned.1.call-update) | async-done | bytes 33554448 | tf_op jit(solution)/shard_map/all_gather | solution.py:206
  544.7 16.4 reduce_sum.157
  573.1 46.6 %all-gather.25.cloned.1.call-done = bf16[2048,1024]{1,0:T(8,128)(2,1)} async-done(((bf16[256,1024]{1,0:T(8,128)(2,1)}), bf16[2048,1024]{1,0:T(8,128)(2,1)}) %all-gather.25.cloned.1.call-update) | async-done | bytes 4194320 | tf_op jit(solution)/shard_map/all_gather | solution.py:156
  619.7 10.0 fusion.64
  629.6 63.5 %all-gather.27.cloned.1.call-done = bf16[2048,1024]{1,0:T(8,128)(2,1)} async-done(((bf16[256,1024]{1,0:T(8,128)(2,1)}), bf16[2048,1024]{1,0:T(8,128)(2,1)}) %all-gather.27.cloned.1.call-update) | async-done | bytes 4194320 | tf_op jit(solution)/shard_map/all_gather | solution.py:157
  693.1 10.0 fusion.65
  703.2 65.2 %all-gather.29.cloned.1.call-done = bf16[1024,2048]{1,0:T(8,128)(2,1)} async-done(((bf16[1024,256]{1,0:T(8,128)(2,1)}), bf16[1024,2048]{1,0:T(8,128)(2,1)}) %all-gather.29.cloned.1.call-update) | async-done | bytes 4194320 | tf_op jit(solution)/shard_map/all_gather | solution.py:158
  768.4 12.8 multiply_convert_fusion.3
  785.8 6.9 convolution_add_fusion
  793.0 9.4 convolution_convert_fusion
  802.4 141.5 %all-reduce.9.cloned.1.call-done = f32[1024,2048]{1,0:T(8,128)} async-done(((f32[1024,2048]{1,0:T(8,128)}), f32[1024,2048]{1,0:T(8,128)}) %all-reduce.9.cloned.1.call-update) | async-done | bytes 8388624 | tf_op jit(solution)/shard_map/psum | solution.py:256
  944.0 8.3 multiply_reduce_fusion
  952.3 7.5 multiply_add_fusion
  960.0 13.0 multiply_convert_fusion
  1007.3 6.9 fusion.68
  1014.2 6.9 fusion.69
  1021.0 11.4 add_convert_fusion
  1032.6 6.7 fusion.71
  1040.6 6.5 fusion.70
  1048.8 9.1 fusion.74
  1059.5 9.1 fusion.75
  1070.3 8.8 fusion.76
  1080.8 10.1 fusion.29
  1092.5 9.1 fusion.72
  1103.1 9.1 fusion.73
  1114.1 71.5 %all-reduce.11.cloned.1.call-done = (bf16[1024,2048]{1,0:T(8,128)(2,1)}, bf16[1024,2048]{1,0:T(8,128)(2,1)}) async-done(((bf16[1024,2048]{1,0:T(8,128)(2,1)}, bf16[1024,2048]{1,0:T(8,128)(2,1)}), (bf16[1024,2048]{1,0:T(8,128)(2,1)}, bf16[1024,2048]{1,0:T(8,128)(2,1)})) %all-reduce.11.cloned.1.call-update) | async-done | bytes 8388624 | tf_op jit(solution)/shard_map/psum | solution.py:217
  1191.9 39.5 %all-reduce.4 = (f32[2048]{0:T(1024)S(1)}, f32[2048]{0:T(1024)S(1)}, f32[2048]{0:T(1024)S(1)}, f32[2048]{0:T(1024)S(1)}) all-reduce(f32[2048]{0:T(1024)S(1)} %get-tuple-element.68, f32[2048]{0:T(1024)S(1)} %get-tuple-element.72, f32[2048]{0:T(1024)S(1)} %copy-done.48, ...), channel_id=11, replica_groups=mesh['dp'=8,'tensor'=4] {'dp'}, use_global_device_ids=true, to_apply=%region_25.26.clone | all-reduce | flops 8192 | bytes 65536
  1233.9 8.5 add_convert_fusion.1
  1242.4 7.4 fusion.11
  1249.8 28.9 %reduce-scatter.11.cloned.1.call-done = f32[256,512]{1,0:T(8,128)} async-done(((f32[2048,512]{1,0:T(8,128)}), f32[256,512]{1,0:T(8,128)}) %reduce-scatter.11.cloned.1.call-update) | async-done | bytes 524304 | tf_op jit(solution)/shard_map/reduce_scatter | solution.py:306
  1278.7 92.2 %reduce-scatter.9.cloned.1.call-done = f32[256,512]{1,0:T(8,128)} async-done(((f32[2048,512]{1,0:T(8,128)}), f32[256,512]{1,0:T(8,128)}) %reduce-scatter.9.cloned.1.call-update) | async-done | bytes 524304 | tf_op jit(solution)/shard_map/reduce_scatter | solution.py:305
  1370.9 151.2 %reduce-scatter.19.cloned.1.call-done = f32[256,1024]{1,0:T(8,128)} async-done(((f32[2048,1024]{1,0:T(8,128)}), f32[256,1024]{1,0:T(8,128)}) %reduce-scatter.19.cloned.1.call-update) | async-done | bytes 1048592 | tf_op jit(solution)/shard_map/reduce_scatter | solution.py:310
  1522.1 150.6 %reduce-scatter.21.cloned.1.call-done = f32[256,1024]{1,0:T(8,128)} async-done(((f32[2048,1024]{1,0:T(8,128)}), f32[256,1024]{1,0:T(8,128)}) %reduce-scatter.21.cloned.1.call-update) | async-done | bytes 1048592 | tf_op jit(solution)/shard_map/reduce_scatter | solution.py:311
  1672.7 151.0 %reduce-scatter.23.cloned.1.call-done = f32[1024,256]{1,0:T(8,128)} async-done(((f32[1024,2048]{1,0:T(8,128)}), f32[1024,256]{1,0:T(8,128)}) %reduce-scatter.23.cloned.1.call-update) | async-done | bytes 1048592 | tf_op jit(solution)/shard_map/reduce_scatter | solution.py:312
  1823.7 151.1 %reduce-scatter.17.cloned.1.call-done = f32[1024,256]{1,0:T(8,128)} async-done(((f32[1024,2048]{1,0:T(8,128)}), f32[1024,256]{1,0:T(8,128)}) %reduce-scatter.17.cloned.1.call-update) | async-done | bytes 1048592 | tf_op jit(solution)/shard_map/reduce_scatter | solution.py:309
  1974.8 150.7 %reduce-scatter.13.cloned.1.call-done = f32[256,1024]{1,0:T(8,128)} async-done(((f32[2048,1024]{1,0:T(8,128)}), f32[256,1024]{1,0:T(8,128)}) %reduce-scatter.13.cloned.1.call-update) | async-done | bytes 1048592 | tf_op jit(solution)/shard_map/reduce_scatter | solution.py:307
  2125.5 150.8 %reduce-scatter.15.cloned.1.call-done = f32[256,1024]{1,0:T(8,128)} async-done(((f32[2048,1024]{1,0:T(8,128)}), f32[256,1024]{1,0:T(8,128)}) %reduce-scatter.15.cloned.1.call-update) | async-done | bytes 1048592 | tf_op jit(solution)/shard_map/reduce_scatter | solution.py:308
  (252 shorter events, 129.2 us)
Async XLA Ops:
  7.2 58.0 %all-gather.19.cloned.1.call-start = ((), (), s32[]{:S(2)}) async-start(), calls=%async_computation.10 | async-start | bytes 2359296 | tf_op jit(solution)/shard_map/all_gather | solution.py:151
  7.9 104.0 %all-gather.21.cloned.1.call-start = ((), (), s32[]{:S(2)}) async-start(), calls=%async_computation.11 | async-start | bytes 2359296 | tf_op jit(solution)/shard_map/all_gather | solution.py:152
  8.7 176.8 %all-gather.17.cloned.1.call-start = ((), (), s32[]{:S(2)}) async-start(), calls=%async_computation.9 | async-start | bytes 4718592 | tf_op jit(solution)/shard_map/all_gather | solution.py:153
  9.4 249.4 %all-gather.15.cloned.1.call-start = ((), (), s32[]{:S(2)}) async-start(), calls=%async_computation.8 | async-start | bytes 4718592 | tf_op jit(solution)/shard_map/all_gather | solution.py:154
  10.0 323.9 %all-gather.23.cloned.1.call-start = ((), (), s32[]{:S(2)}) async-start(), calls=%async_computation.12 | async-start | bytes 4718592 | tf_op jit(solution)/shard_map/all_gather | solution.py:155
  10.6 534.2 %all-gather.31.cloned.1.call-start = ((), (), s32[]{:S(2)}) async-start(), calls=%async_computation.25 | async-start | bytes 41943040 | tf_op jit(solution)/shard_map/all_gather | solution.py:206
  10.6 4.9 copy-start.1
  15.5 25.8 %copy-start.57 = (bf16[256]{0:T(256)(128)(2,1)S(1)}, bf16[256]{0:T(256)(128)(2,1)}, u32[]{:S(2)}) copy-start(bf16[256]{0:T(256)(128)(2,1)} %param.26) | copy-start | bytes 1540
  15.5 46.3 %copy-start.44 = (f32[1024]{0:T(1024)}, f32[1024]{0:T(1024)S(1)}, u32[]{:S(2)}) copy-start(f32[1024]{0:T(1024)S(1)} %broadcast_multiply_fusion.9) | copy-start | bytes 12292
  16.8 45.1 %copy-start.46 = (f32[1024]{0:T(1024)}, f32[1024]{0:T(1024)S(1)}, u32[]{:S(2)}) copy-start(f32[1024]{0:T(1024)S(1)} %add_rsqrt_fusion.2) | copy-start | bytes 12292
  17.0 106.9 %copy-start.14 = (f32[1024,128]{1,0:T(8,128)}, f32[1024,128]{1,0:T(8,128)S(1)}, u32[]{:S(2)}) copy-start(f32[1024,128]{1,0:T(8,128)S(1)} %get-tuple-element.103) | copy-start | bytes 1572868
  17.0 106.9 %copy-start.16 = (f32[1024,128]{1,0:T(8,128)}, f32[1024,128]{1,0:T(8,128)S(1)}, u32[]{:S(2)}) copy-start(f32[1024,128]{1,0:T(8,128)S(1)} %get-tuple-element.104) | copy-start | bytes 1572868
  19.0 105.0 %copy-start.18 = (f32[1024,128]{1,0:T(8,128)}, f32[1024,128]{1,0:T(8,128)S(1)}, u32[]{:S(2)}) copy-start(f32[1024,128]{1,0:T(8,128)S(1)} %get-tuple-element.105) | copy-start | bytes 1572868
  19.0 105.0 %copy-start.20 = (f32[1024,128]{1,0:T(8,128)}, f32[1024,128]{1,0:T(8,128)S(1)}, u32[]{:S(2)}) copy-start(f32[1024,128]{1,0:T(8,128)S(1)} %get-tuple-element.106) | copy-start | bytes 1572868
  41.3 20.5 copy-start.42
  185.4 8.6 copy-start.26
  344.8 20.1 copy-start.59
  344.9 274.8 %all-gather.25.cloned.1.call-start = ((), (), s32[]{:S(2)}) async-start(), calls=%async_computation.13 | async-start | bytes 4718592 | tf_op jit(solution)/shard_map/all_gather | solution.py:156
  345.6 347.5 %all-gather.27.cloned.1.call-start = ((), (), s32[]{:S(2)}) async-start(), calls=%async_computation.14 | async-start | bytes 4718592 | tf_op jit(solution)/shard_map/all_gather | solution.py:157
  346.4 422.0 %all-gather.29.cloned.1.call-start = ((), (), s32[]{:S(2)}) async-start(), calls=%async_computation.15 | async-start | bytes 4718592 | tf_op jit(solution)/shard_map/all_gather | solution.py:158
  347.1 596.9 %all-reduce.9.cloned.1.call-start = ((), (), s32[]{:S(2)}) async-start(), calls=%async_computation.16 | async-start | bytes 16777216 | tf_op jit(solution)/shard_map/psum | solution.py:256
  768.4 12.8 copy-start.52
  781.2 4.6 copy-start.64
  781.2 4.6 copy-start.53
  792.8 392.8 %all-reduce.11.cloned.1.call-start = ((), (), s32[]{:S(2)}) async-start(), calls=%async_computation.26 | async-start | bytes 16777216 | tf_op jit(solution)/shard_map/psum | solution.py:217
  944.0 8.3 copy-start.23
  952.3 7.5 copy-start.5
  952.3 7.7 copy-start.6
  959.8 13.2 copy-start.3
  978.9 6.4 copy-start.8
  992.5 7.6 copy-start.9
  1007.3 6.9 copy-start.22
  1007.3 6.9 copy-start.24
  1032.4 246.3 %reduce-scatter.11.cloned.1.call-start = ((), (), s32[]{:S(2)}) async-start(), calls=%async_computation.18 | async-start | bytes 4718592 | tf_op jit(solution)/shard_map/reduce_scatter | solution.py:306
  1039.4 331.5 %reduce-scatter.9.cloned.1.call-start = ((), (), s32[]{:S(2)}) async-start(), calls=%async_computation.17 | async-start | bytes 4718592 | tf_op jit(solution)/shard_map/reduce_scatter | solution.py:305
  1047.1 474.9 %reduce-scatter.19.cloned.1.call-start = ((), (), s32[]{:S(2)}) async-start(), calls=%async_computation.22 | async-start | bytes 9437184 | tf_op jit(solution)/shard_map/reduce_scatter | solution.py:310
  1057.9 614.8 %reduce-scatter.21.cloned.1.call-start = ((), (), s32[]{:S(2)}) async-start(), calls=%async_computation.23 | async-start | bytes 9437184 | tf_op jit(solution)/shard_map/reduce_scatter | solution.py:311
  1068.7 755.1 %reduce-scatter.23.cloned.1.call-start = ((), (), s32[]{:S(2)}) async-start(), calls=%async_computation.24 | async-start | bytes 9437184 | tf_op jit(solution)/shard_map/reduce_scatter | solution.py:312
  1079.2 895.6 %reduce-scatter.17.cloned.1.call-start = ((), (), s32[]{:S(2)}) async-start(), calls=%async_computation.21 | async-start | bytes 9437184 | tf_op jit(solution)/shard_map/reduce_scatter | solution.py:309
  1090.9 1034.6 %reduce-scatter.13.cloned.1.call-start = ((), (), s32[]{:S(2)}) async-start(), calls=%async_computation.19 | async-start | bytes 9437184 | tf_op jit(solution)/shard_map/reduce_scatter | solution.py:307
  1101.6 1174.7 %reduce-scatter.15.cloned.1.call-start = ((), (), s32[]{:S(2)}) async-start(), calls=%async_computation.20 | async-start | bytes 9437184 | tf_op jit(solution)/shard_map/reduce_scatter | solution.py:308
  1112.2 73.4 %copy-start.43 = (f32[8,1,256]{2,1,0:T(1,128)S(1)}, f32[8,1,256]{2,1,0:T(1,128)}, u32[]{:S(2)}) copy-start(f32[8,1,256]{2,1,0:T(1,128)} %copy-done.42) | copy-start | bytes 24580
  1112.2 73.4 %copy-start.45 = (f32[1024]{0:T(1024)S(1)}, f32[1024]{0:T(1024)}, u32[]{:S(2)}) copy-start(f32[1024]{0:T(1024)} %copy-done.44) | copy-start | bytes 12292
  1112.2 73.4 %copy-start.47 = (f32[1024]{0:T(1024)S(1)}, f32[1024]{0:T(1024)}, u32[]{:S(2)}) copy-start(f32[1024]{0:T(1024)} %copy-done.46) | copy-start | bytes 12292
  1185.6 6.2 copy-start.48
  1185.6 6.2 copy-start.49
  1233.9 8.5 copy-start.2
  1233.9 8.5 copy-start.7
  (39 other events, 92.8 us)
Sparse Core Ops, SparseCore 0:
  10.1 52.0 all-gather.18
  64.3 47.5 all-gather.20
  114.1 71.3 all-gather.16
  187.4 71.3 all-gather.14
  260.6 73.1 all-gather.22
  345.0 199.6 all-gather.30
  546.8 72.7 all-gather.24
  621.8 71.3 all-gather.26
  695.2 73.1 all-gather.28
  792.9 151.0 all-reduce.8
  1032.5 153.0 all-reduce.10
  1189.7 88.9 reduce-scatter.10
  1282.9 87.9 reduce-scatter.8
  1374.9 147.0 reduce-scatter.18
  1526.1 146.5 reduce-scatter.20
  1676.8 146.9 reduce-scatter.22
  1827.8 146.9 reduce-scatter.16
  1978.9 146.5 reduce-scatter.12
  2129.7 146.5 reduce-scatter.14
